TPU v7x, 128 devices: a whole 4x4x4 slice. The times are simulated.
128 devices in a mesh: dp: 8 (over y, core), feat: 16 (over z, x).
Axes of the slice: x: 4, y: 4, z: 4, core: 2. Of those that a mesh axis runs over, the one named last changes fastest.
Arguments:
- features: bfloat16 [32768, 8192], P('dp', 'feat'), may hold values from -6 to 6
- fixed_coef: float32 [8192], P('feat'), may hold values from -0.0625 to 0.0625
- member_score: float32 [32768], P('dp'), may hold values from -6 to 6
- clicks: int32 [32768], P('dp'), may hold values 0 or 1
- member_features: bfloat16 [32768, 256], P(('dp', 'feat')), may hold values from -6 to 6
- member_coef: float32 [1024, 256], P(('dp', 'feat')), may hold values from -0.375 to 0.375
- block_slot: int32 [32768], P(('dp', 'feat')), may hold values from 0 to 65535, as said below
Outputs:
- fixed_grad: float32 [8192], P('feat')
- member_coef_new: float32 [1024, 256], P(('dp', 'feat'))
- total_score: float32 [32768], P(('dp', 'feat'))
Inputs may be any that keep to these rules, and one draw needn't show every extreme that they name: All block_slot values differ. block_slot // 512 is the device (index along dp+feat) that owns the impression's member, and block_slot // 64 is the member. Every owner receives exactly 256 impressions. One device sends at most 6 of its impressions to one owner, and every device sends exactly 6 to some owner.
All inputs are finite; a program needn't handle non-finite values. Where the computation divides by a largest or mean magnitude, that divisor is 1e-20 or more. No bound on the sum of `clicks` on one device may be relied on, other than what follows from the above.
Results may differ from a plain program's by a relative error of at most 0.0093.
Values may be sent and summed in bfloat16 or wider, within the bound.
A program may use at most 64 MiB of HBM per device.

v0:
```python
import math

import jax
import jax.numpy as jnp
from jax import lax
from jax.sharding import PartitionSpec as P

BLK = 64
NEWTON = 3


ridge_weight = 1.0
high = lax.Precision.HIGHEST
inverse_sweeps = 20


def apply_inverse(system, vector):
    identity = jnp.eye(system.shape[1], dtype=system.dtype)
    bound = jnp.max(jnp.sum(jnp.abs(system), axis=2), axis=1)
    start = (2.0 / (1.0 + bound))[:, None, None] * identity[None, :, :]

    def sweep(index, approx):
        product = jnp.einsum("mbc,mcd->mbd", system, approx, precision=high)
        return 2.0 * approx - jnp.einsum("mbc,mcd->mbd", approx, product, precision=high)

    approx = lax.fori_loop(0, inverse_sweeps, sweep, start)
    return jnp.einsum("mbc,mc->mb", approx, vector, precision=high)


def newton_blocks(padded_rows, offset, label_pad, live_pad, coeffs):
    gram_matrix = jnp.einsum("mbk,mck->mbc", padded_rows, padded_rows, precision=high)
    identity = jnp.eye(padded_rows.shape[1], dtype=padded_rows.dtype)
    for iteration in range(NEWTON):
        linear = offset + jnp.einsum("mbk,mk->mb", padded_rows, coeffs, precision=high)
        probability = jax.nn.sigmoid(linear)
        gradient = (
            jnp.einsum(
                "mbk,mb->mk", padded_rows, live_pad * (probability - label_pad), precision=high
            )
            + ridge_weight * coeffs
        )
        weight_root = jnp.sqrt(live_pad * probability * (1.0 - probability))
        system = (
            ridge_weight * identity
            + weight_root[:, :, None] * gram_matrix * weight_root[:, None, :]
        )
        projected = weight_root * jnp.einsum("mbk,mk->mb", padded_rows, gradient, precision=high)
        solved = apply_inverse(system, projected)
        back_term = jnp.einsum("mbk,mb->mk", padded_rows, weight_root * solved, precision=high)
        coeffs = coeffs - (gradient - back_term) / ridge_weight
    return coeffs


def per_device(
    features, fixed_coef, member_score, clicks, member_features, member_coef, block_slot
):
    n_dp = lax.axis_size("dp")
    n_feat = lax.axis_size("feat")
    devices = n_dp * n_feat
    rows_own = member_features.shape[0]
    width = member_features.shape[1]
    slot_count = 2 * rows_own
    blocks = slot_count // BLK
    capacity = 3 * ((rows_own + devices - 1) // devices)
    row_start = lax.axis_index("feat") * rows_own
    coef_half = fixed_coef.astype(jnp.bfloat16)
    partial_score = jnp.dot(features, coef_half, preferred_element_type=jnp.float32)
    own_clicks = lax.dynamic_slice_in_dim(clicks, row_start, rows_own).astype(jnp.float32)
    fixed_score = lax.psum(partial_score, "feat")
    residual = (jax.nn.sigmoid(fixed_score + member_score) - clicks.astype(jnp.float32)).astype(
        jnp.bfloat16
    )
    own_score = lax.dynamic_slice_in_dim(fixed_score, row_start, rows_own)
    grad_part = jnp.dot(residual, features, preferred_element_type=jnp.float32)
    fixed_grad = lax.psum(grad_part, "dp") / math.sqrt(rows_own * devices)
    owner_dev = block_slot // slot_count
    local_slot = block_slot - owner_dev * slot_count
    onehot = (owner_dev[:, None] == jnp.arange(devices, dtype=jnp.int32)[None, :]).astype(jnp.int32)
    row_rank = jnp.sum(jnp.cumsum(onehot, axis=0) * onehot, axis=1) - 1
    send_place = owner_dev * capacity + row_rank
    rows_out = (
        jnp.zeros((devices * capacity, width), jnp.bfloat16).at[send_place].set(member_features)
    )
    tag_value = (local_slot * 2).astype(jnp.float32) + own_clicks
    score_buffer = jnp.zeros((devices * capacity,), jnp.float32).at[send_place].set(own_score)
    tag_buffer = jnp.full((devices * capacity,), -1.0, jnp.float32).at[send_place].set(tag_value)
    meta_out = jnp.stack([score_buffer, tag_buffer])
    rows_in = lax.all_to_all(
        rows_out.reshape(devices, capacity, width),
        ("dp", "feat"),
        split_axis=0,
        concat_axis=0,
        tiled=True,
    )
    meta_in = lax.all_to_all(
        meta_out.reshape(2, devices, capacity),
        ("dp", "feat"),
        split_axis=1,
        concat_axis=1,
        tiled=True,
    )
    rows_in = rows_in.reshape(devices * capacity, width)
    meta_in = meta_in.reshape(2, devices * capacity)
    tags_in = meta_in[1]
    valid_slot = tags_in >= 0.0
    tag_int = jnp.where(valid_slot, tags_in, 0.0).astype(jnp.int32)
    label_in = (tag_int % 2).astype(jnp.float32)
    where_local = jnp.where(valid_slot, tag_int // 2, slot_count)
    padded_rows = (
        jnp.zeros((slot_count + 1, width), jnp.float32)
        .at[where_local]
        .set(rows_in.astype(jnp.float32))[:slot_count]
        .reshape(blocks, BLK, width)
    )
    offset = (
        jnp.zeros((slot_count + 1,), jnp.float32)
        .at[where_local]
        .set(meta_in[0])[:slot_count]
        .reshape(blocks, BLK)
    )
    label_pad = (
        jnp.zeros((slot_count + 1,), jnp.float32)
        .at[where_local]
        .set(label_in)[:slot_count]
        .reshape(blocks, BLK)
    )
    live_pad = (
        jnp.zeros((slot_count + 1,), jnp.float32)
        .at[where_local]
        .set(1.0)[:slot_count]
        .reshape(blocks, BLK)
    )
    coeffs = newton_blocks(padded_rows, offset, label_pad, live_pad, member_coef)
    member_value = jnp.einsum("mbk,mk->mb", padded_rows, coeffs, precision=high).reshape(slot_count)
    back_value = jnp.where(valid_slot, member_value[jnp.minimum(where_local, slot_count - 1)], 0.0)
    returned = lax.all_to_all(
        back_value.reshape(devices, capacity),
        ("dp", "feat"),
        split_axis=0,
        concat_axis=0,
        tiled=True,
    )
    returned = returned.reshape(devices * capacity)
    total_score = own_score + returned[send_place]
    return (fixed_grad, coeffs, total_score)


def solution(mesh):
    return jax.shard_map(
        per_device,
        mesh=mesh,
        in_specs=(
            P("dp", "feat"),
            P("feat"),
            P("dp"),
            P("dp"),
            P(("dp", "feat"), None),
            P(("dp", "feat"), None),
            P(("dp", "feat")),
        ),
        out_specs=(P("feat"), P(("dp", "feat"), None), P(("dp", "feat"))),
        check_vma=False,
    )
```

profile of v0, /device:TPU:1, one launch (start us, length us, event | category | flops | bytes accessed | tf_op | source)
XLA Modules:
  0.0 235.6 jit_solution(464150204069671483)
XLA Ops:
  0.7 0.8 convert_add_fusion
  2.1 0.7 convert_element_type.65
  2.8 3.4 %fusion.54 = f32[1,4096]{1,0:T(1,128)S(1)} fusion(bf16[4096,512]{1,0:T(8,128)(2,1)} %param.13, bf16[512,1]{0,1:T(2,128)(2,1)S(1)} %reshape.293), kind=kOutput, calls=%fused_computation.124 | convolution fusion | flops 4194304 | bytes 4211712 | tf_op jit(solution)/shard_map/dot_general | solution.py:67
  6.1 62.3 %psum.14 = f32[4096]{0:T(1024)S(1)} all-reduce(f32[4096]{0:T(1024)S(1)} %bitcast.212), channel_id=1, replica_groups=mesh['dp'=8,'feat'=16] {'feat'}, use_global_device_ids=true, to_apply=%region_0.0 | all-reduce | flops 4096 | bytes 32768 | tf_op jit(solution)/shard_map/psum | solution.py:69
  68.5 1.4 scatter_custom_fusion
  70.0 1.4 scatter_custom_fusion.1
  71.6 0.8 copy.54
  72.3 18.9 %all-to-all-start = ((f32[2,128,6]{2,0,1:T(2,128)}), f32[2,128,6]{2,0,1:T(2,128)S(1)}, u32[]{:S(2)}, u32[]{:S(2)}) async-start(f32[2,128,6]{2,0,1:T(2,128)} %copy.54), calls=%async_computation | async-start | bytes 262144 | tf_op jit(solution)/shard_map/all_to_all | solution.py:95
  91.3 2.8 %fusion.55 = f32[1,512]{1,0:T(1,128)S(1)} fusion(bf16[4096,1]{0,1:T(2,128)(2,1)S(1)} %reshape.295, bf16[4096,512]{1,0:T(8,128)(2,1)} %param.13), kind=kOutput, calls=%fused_computation.125 | convolution fusion | flops 4194304 | bytes 4204544 | tf_op jit(solution)/shard_map/dot_general | solution.py:74
  94.2 12.8 %psum.15 = f32[512]{0:T(512)S(1)} all-reduce(f32[512]{0:T(512)S(1)} %bitcast.239), channel_id=1, replica_groups=mesh['dp'=8,'feat'=16] {'dp'}, use_global_device_ids=true, to_apply=%region_1.0 | all-reduce | flops 512 | bytes 4096 | tf_op jit(solution)/shard_map/psum | solution.py:75
  107.0 0.6 broadcast_multiply_fusion.3
  107.6 2.0 scatter_custom_fusion.2
  109.6 0.9 reshape.209
  110.5 9.4 %all-to-all-start.1 = ((bf16[128,6,256]{2,1,0:T(8,128)(2,1)}), bf16[128,6,256]{2,1,0:T(8,128)(2,1)S(1)}, u32[]{:S(2)}, u32[]{:S(2)}) async-start(bf16[128,6,256]{2,1,0:T(8,128)(2,1)} %reshape.209), calls=%async_computation.1 | async-start | bytes 1048576 | tf_op jit(solution)/shard_map/all_to_all | solution.py:88
  120.5 3.4 %scatter_custom_fusion.6 = f32[513]{0:T(1024)S(1)} fusion(s32[768]{0:T(1024)S(1)} %get-tuple-element.94, f32[768]{0:T(1024)S(1)} %fusion.33, f32[]{:T(128)} %constant.51.clone.1), kind=kCustom, calls=%fused_computation.98 | custom fusion | bytes 2056 | tf_op jit(solution)/shard_map/scatter | solution.py:124
  124.1 3.4 %scatter_custom_fusion.5 = f32[513]{0:T(1024)S(1)} fusion(s32[768]{0:T(1024)S(1)} %get-tuple-element.94, f32[768]{0:T(1024)S(1)} %reshape.277, f32[]{:T(128)} %constant.51.clone.1), kind=kCustom, calls=%fused_computation.100 | custom fusion | bytes 2056 | tf_op jit(solution)/shard_map/scatter | solution.py:118
  127.6 3.6 %scatter_custom_fusion.4 = f32[513]{0:T(1024)S(1)} fusion(s32[768]{0:T(1024)S(1)} %get-tuple-element.94, f32[768]{0:T(1024)S(1)} %broadcast.285, f32[]{:T(128)} %constant.51.clone.1), kind=kCustom, calls=%fused_computation.102 | custom fusion | bytes 2056 | tf_op jit(solution)/shard_map/scatter | solution.py:130
  131.2 2.8 %all-to-all-done.1 = bf16[128,6,256]{2,1,0:T(8,128)(2,1)S(1)} async-done(((bf16[128,6,256]{2,1,0:T(8,128)(2,1)}), bf16[128,6,256]{2,1,0:T(8,128)(2,1)S(1)}, u32[]{:S(2)}, u32[]{:S(2)}) %all-to-all-start.1) | async-done | bytes 393248 | tf_op jit(solution)/shard_map/all_to_all | solution.py:88
  134.1 5.6 %scatter_custom_fusion.3 = f32[513,256]{1,0:T(8,128)S(1)} fusion(s32[768]{0:T(1024)S(1)} %get-tuple-element.94, f32[768,256]{1,0:T(8,128)S(1)} %reshape.261, f32[]{:T(128)} %constant.51.clone.1), kind=kCustom, calls=%fused_computation.15 | custom fusion | bytes 525316 | tf_op jit(solution)/shard_map/scatter | solution.py:112
  139.8 0.6 fusion.27
  140.8 0.6 fusion.25
  141.4 0.6 abs_reduce_fusion.2
  142.4 20.0 %while.30 = (s32[]{:T(128)}, f32[8,64,64]{1,2,0:T(8,128)S(1)}, f32[8,64,64]{2,1,0:T(8,128)S(1)}, s32[]{:T(128)}) while((s32[]{:T(128)}, f32[8,64,64]{1,2,0:T(8,128)S(1)}, f32[8,64,64]{2,1,0:T(8,128)S(1)}, s32[]{:T(128)}) %tuple.70), condition=%wide.region_15.16_spmd, body=%wide.region_14.15_spmd.sunk | while | flops 50397184 | bytes 1048629 | solution.py:26
  142.4 0.5 fusion.130
  145.4 0.5 fusion.130
  146.4 0.5 fusion.130
  149.4 0.5 fusion.130
  150.4 0.5 fusion.130
  153.4 0.5 fusion.130
  154.4 0.5 fusion.130
  157.4 0.5 fusion.130
  158.4 0.5 fusion.130
  161.4 0.5 fusion.130
  163.1 0.6 fusion.23
  164.1 0.6 fusion.21
  165.2 20.0 %while.31 = (s32[]{:T(128)}, f32[8,64,64]{1,2,0:T(8,128)S(1)}, f32[8,64,64]{2,1,0:T(8,128)S(1)}, s32[]{:T(128)}) while((s32[]{:T(128)}, f32[8,64,64]{1,2,0:T(8,128)S(1)}, f32[8,64,64]{2,1,0:T(8,128)S(1)}, s32[]{:T(128)}) %tuple.73), condition=%wide.region_19.20_spmd, body=%wide.region_18.19_spmd.sunk | while | flops 50397184 | bytes 1048629 | solution.py:26
  165.3 0.5 fusion.136
  168.3 0.5 fusion.136
  169.3 0.5 fusion.136
  172.3 0.5 fusion.136
  173.3 0.5 fusion.136
  176.3 0.5 fusion.136
  177.3 0.5 fusion.136
  180.3 0.5 fusion.136
  181.3 0.5 fusion.136
  184.3 0.5 fusion.136
  186.0 0.5 fusion.19
  187.0 0.5 fusion.17
  188.1 20.0 %while.32 = (s32[]{:T(128)}, f32[8,64,64]{1,2,0:T(8,128)S(1)}, f32[8,64,64]{2,1,0:T(8,128)S(1)}, s32[]{:T(128)}) while((s32[]{:T(128)}, f32[8,64,64]{1,2,0:T(8,128)S(1)}, f32[8,64,64]{2,1,0:T(8,128)S(1)}, s32[]{:T(128)}) %tuple.76), condition=%wide.region_23.24_spmd, body=%wide.region_22.23_spmd.sunk | while | flops 50397184 | bytes 1048629 | solution.py:26
  190.2 0.5 fusion.142
  193.2 0.5 fusion.142
  194.2 0.5 fusion.142
  197.2 0.5 fusion.142
  198.2 0.5 fusion.142
  201.2 0.5 fusion.142
  202.2 0.5 fusion.142
  208.9 0.5 fusion.15
  209.5 5.0 %gather_fusion = f32[768]{0:T(1024)S(1)} fusion(f32[512]{0:T(512)S(1)} %reshape.214, s32[1024]{0:T(1024)S(1)} %pad_clamp_fusion.1), kind=kCustom, calls=%fused_computation | custom fusion | bytes 9216 | tf_op jit(solution)/shard_map/gather | solution.py:135
  214.7 0.6 bitcast_select_fusion.1
  215.3 7.0 %all-to-all-start.2 = ((f32[128,1,6]{2,1,0:T(1,128)}), f32[128,1,6]{2,1,0:T(1,128)S(1)}, u32[]{:S(2)}, u32[]{:S(2)}) async-start(f32[128,1,6]{2,1,0:T(1,128)} %bitcast.62), calls=%async_computation.2 | async-start | bytes 131072 | tf_op jit(solution)/shard_map/all_to_all | solution.py:136
  222.3 9.8 %all-to-all-done.2 = f32[128,1,6]{2,1,0:T(1,128)S(1)} async-done(((f32[128,1,6]{2,1,0:T(1,128)}), f32[128,1,6]{2,1,0:T(1,128)S(1)}, u32[]{:S(2)}, u32[]{:S(2)}) %all-to-all-start.2) | async-done | bytes 3104 | tf_op jit(solution)/shard_map/all_to_all | solution.py:136
  232.6 0.8 reduce.11
  233.6 1.4 gather_fusion.1
  234.9 0.6 dynamic-slice_add_fusion
  (239 shorter events, 50.8 us)
Async XLA Ops:
  0.6 90.6 %copy-start.2 = (s32[4096]{0:T(1024)S(1)}, s32[4096]{0:T(1024)}, u32[]{:S(2)}) copy-start(s32[4096]{0:T(1024)} %param.16) | copy-start | bytes 49156
  0.6 90.6 %copy-start.3 = (f32[4096]{0:T(1024)S(1)}, f32[4096]{0:T(1024)}, u32[]{:S(2)}) copy-start(f32[4096]{0:T(1024)} %param.15) | copy-start | bytes 49156
  72.3 38.2 %all-to-all-start = ((f32[2,128,6]{2,0,1:T(2,128)}), f32[2,128,6]{2,0,1:T(2,128)S(1)}, u32[]{:S(2)}, u32[]{:S(2)}) async-start(f32[2,128,6]{2,0,1:T(2,128)} %copy.54), calls=%async_computation | async-start | bytes 262144 | tf_op jit(solution)/shard_map/all_to_all | solution.py:95
  91.3 48.4 %copy-start = (f32[8,256]{1,0:T(8,128)S(1)}, f32[8,256]{1,0:T(8,128)}, u32[]{:S(2)}) copy-start(f32[8,256]{1,0:T(8,128)} %param.18) | copy-start | bytes 24580
  110.5 23.5 %all-to-all-start.1 = ((bf16[128,6,256]{2,1,0:T(8,128)(2,1)}), bf16[128,6,256]{2,1,0:T(8,128)(2,1)S(1)}, u32[]{:S(2)}, u32[]{:S(2)}) async-start(bf16[128,6,256]{2,1,0:T(8,128)(2,1)} %reshape.209), calls=%async_computation.1 | async-start | bytes 1048576 | tf_op jit(solution)/shard_map/all_to_all | solution.py:88
  208.9 26.7 %copy-start.1 = (f32[8,256]{1,0:T(8,128)}, f32[8,256]{1,0:T(8,128)S(1)}, u32[]{:S(2)}) copy-start(f32[8,256]{1,0:T(8,128)S(1)} %fusion.12) | copy-start | bytes 24580
  215.3 16.8 %all-to-all-start.2 = ((f32[128,1,6]{2,1,0:T(1,128)}), f32[128,1,6]{2,1,0:T(1,128)S(1)}, u32[]{:S(2)}, u32[]{:S(2)}) async-start(f32[128,1,6]{2,1,0:T(1,128)} %bitcast.62), calls=%async_computation.2 | async-start | bytes 131072 | tf_op jit(solution)/shard_map/all_to_all | solution.py:136
where the time goes:
time: 236 us
  blocking collectives  75.1 us (32%)
  matrix products  70.7 us (30%)
  starting transfers between devices  35.3 us (15%)
  local copies, waits for them, and re-layouts  32.6 us (14%)
  waiting for transfers between devices  12.6 us (5%)
  other arithmetic  5.86 us (2%)
    psum x1, blocking collectives, per_device(): fixed_score = lax.psum(partial_score, 'feat')  62.3 us
    dot_general x60, matrix products, sweep(): product = jnp.einsum('mbc,mcd->mbd', system, approx, precision=high)  32.8 us
    dot_general x60, matrix products, sweep(): jnp.einsum('mbc,mcd->mbd', approx, product, precision=high)  23.8 us
    all_to_all x1, starting transfers between devices, per_device(): lax.all_to_all(meta_out.reshape(2, devices, capacity), ('dp', 'feat'), sp...  18.9 us
    psum x1, blocking collectives, per_device(): fixed_grad = lax.psum(grad_part, 'dp') / math.sqrt(rows_own * devices)  12.8 us
    all_to_all x1, waiting for transfers between devices, per_device(): lax.all_to_all(back_value.reshape(devices, capacity), ('dp', 'feat'), spl...  9.8 us
    all_to_all x1, starting transfers between devices, per_device(): lax.all_to_all(rows_out.reshape(devices, capacity, width), ('dp', 'feat')...  9.4 us
    all_to_all x1, starting transfers between devices, per_device(): lax.all_to_all(back_value.reshape(devices, capacity), ('dp', 'feat'), spl...  6.99 us
  transfers between devices with their start and end apart: 3, of which 2 were waited for; matrix products, arithmetic and copies ran while one was open for 7% of the time, Pallas kernels for 0%

commit v1 on v0

v1 whole, which is shorter than its diff:
```python
import math

import jax
import jax.numpy as jnp
from jax import lax
from jax.experimental import pallas as pl
from jax.experimental.pallas import tpu as pltpu
from jax.sharding import PartitionSpec as P

MESH = pl.DeviceIdType.MESH
BLK = 64
NEWTON = 3
PAIRS = 4
f32, bf16, i32 = jnp.float32, jnp.bfloat16, jnp.int32


def iota(shape, dim):
    return lax.broadcasted_iota(i32, shape, dim)


def dot(a, b):
    return lax.dot_general(a, b, (((1,), (0,)), ((), ())), preferred_element_type=f32)


def dot_nt(a, b):
    return lax.dot_general(a, b, (((1,), (1,)), ((), ())), preferred_element_type=f32)


def split3(x):
    high = x.astype(bf16)
    rest = x - high.astype(f32)
    mid = rest.astype(bf16)
    low = (rest - mid.astype(f32)).astype(bf16)
    return high, mid, low


def stack3(x):
    return jnp.concatenate([t.astype(f32) for t in split3(x)], axis=0).astype(bf16)


def fold3(y):
    n = y.shape[0] // 3
    return (y[:n] + y[n : 2 * n]) + y[2 * n :]


def onehot(mask):
    return jnp.where(mask, 1.0, 0.0).astype(bf16)


def two_rows(x):
    return jnp.concatenate([x[0:1], x[1:2]], axis=1)


def take(x, index):
    return jnp.take_along_axis(x, index, axis=1, mode="promise_in_bounds")


def solve(rows, y):
    lane = iota((8, 128), 1)
    low = lane < 64
    col = lane & 63
    rows = list(rows)
    s = jnp.zeros((8, 128), f32)
    for q in range(0, 32, PAIRS):
        raw, vars_, offs, pivots = [], [], [], []
        for p in range(q, q + PAIRS):
            rolled = pltpu.roll(rows[p], 64, 1)
            raw += [rows[p], rows[p]]
            offs += [0, 64]
            vars_ += [p, p + 32]
            pivots += [jnp.where(low, rows[p], rolled), jnp.where(low, rolled, rows[p])]
        n = len(vars_)
        block = {
            (i, j): jnp.broadcast_to(
                raw[i][:, offs[i] + vars_[j] : offs[i] + vars_[j] + 1], (8, 128)
            )
            for i in range(n)
            for j in range(i, n)
        }
        ys = [jnp.broadcast_to(y[:, v : v + 1], (8, 128)) for v in vars_]
        half = col & 31
        inside = (half >= q) & (half < q + PAIRS)
        done = half < q + PAIRS
        t = [
            jnp.where(col == vars_[i], 1.0, jnp.where(inside, 0.0, pivots[i])) for i in range(n)
        ]
        inv, factor = [], {}
        for k in range(n):
            inv.append(1.0 / block[k, k])
            for i in range(k + 1, n):
                factor[i, k] = block[k, i] * inv[k]
            for i in range(k + 1, n):
                t[i] = t[i] - factor[i, k] * t[k]
                for j in range(i, n):
                    block[i, j] = block[i, j] - factor[i, k] * block[k, j]
        t = [t[i] * inv[i] for i in range(n)]
        for k in range(n - 1, 0, -1):
            for i in range(k):
                t[i] = t[i] - factor[k, i] * t[k]
        step = ys[0] * t[0]
        for i in range(1, n):
            step = step + ys[i] * t[i]
        s = s + jnp.where(done, step, 0.0)
        y = y - jnp.where(done, 0.0, step)
        for p in range(q + PAIRS, 32):
            pick = [jnp.where(low, off + p, off + p + 32) for off in (0, 64)]
            new = jnp.where(inside, 0.0, rows[p])
            for i in range(n):
                new = new - take(raw[i], pick[i % 2]) * t[i]
            rows[p] = new
    return s


def gram_times(gram_ref, v):
    low = iota((8, 128), 1) < 64
    total = jnp.zeros((8, 128), f32)
    for p in range(32):
        total = total + gram_ref[8 * p : 8 * p + 8, :] * take(v, jnp.where(low, p, p + 32))
    return total + pltpu.roll(total, 64, 1)


def kernel(
    coef_ref, mscore_ref, click_ref, mfeat_ref, mcoef_ref, slot_ref, feat_ref,
    grad_ref, coefs_ref, total_ref,
    fbuf, msg, rin, part, rs, own, ag, sc, scr, bk, ret, gsrc, gin,
    owner_hot, lane_of, rows_src, bhot, padded, gram,
    fsem, ssem, rsem,
):
    n_dp, n_feat = 8, 16
    n_dev = n_dp * n_feat
    dp, feat = lax.axis_index("dp"), lax.axis_index("feat")
    me = dp * n_feat + feat

    chunks = 8
    rows_chunk = fbuf.shape[0] // chunks

    def feature_copy(c):
        window = pl.ds(c * rows_chunk, rows_chunk)
        return pltpu.make_async_copy(feat_ref.at[window], fbuf.at[window], fsem.at[c])

    for c in range(chunks):
        feature_copy(c).start()

    barrier = pltpu.get_barrier_semaphore()

    def device(t):
        return (t // n_feat, lax.rem(t, n_feat))

    def others(n, body):
        def step(d, carry):
            body(d)
            return carry

        lax.fori_loop(1, n, step, 0)

    def hello(d):
        t = lax.rem(me + d, n_dev)
        pl.semaphore_signal(barrier, inc=1, device_id=device(t), device_id_type=MESH)

    others(n_dev, hello)

    def send(src, dst, which, target):
        return pltpu.make_async_remote_copy(
            src_ref=src, dst_ref=dst, send_sem=ssem.at[which], recv_sem=rsem.at[which],
            device_id=target, device_id_type=MESH,
        )

    def arrived(ref, which):
        send(ref, ref, which, (dp, feat)).wait_recv()

    def sent(ref, which):
        send(ref, ref, which, (dp, feat)).wait_send()

    slots = slot_ref[...]
    owner = slots >> 9
    own_clicks = two_rows(click_ref[pl.ds(2 * feat, 2), :])
    tag = (slots & 511) * 2 + own_clicks + 1
    hot = iota((n_dev, 256), 0) == owner
    hot_half = onehot(hot)
    before = onehot(iota((256, 256), 0) < iota((256, 256), 1))
    counts = dot(hot_half, before)
    rank = jnp.sum(jnp.where(hot, counts, 0.0), axis=0, keepdims=True).astype(i32)
    lane_row = rank + feat * 8
    owner_hot[...] = hot_half
    lane_of[...] = lane_row
    place = owner * 8 + rank
    lane_hot = iota((128, 256), 0) == lane_row

    def by_owner(row):
        return dot_nt(hot_half, jnp.where(lane_hot, row, 0.0).astype(bf16))

    tags = jnp.concatenate(
        [by_owner((tag >> 5).astype(f32)), by_owner((tag & 31).astype(f32))], axis=1
    ).astype(bf16)

    def pack(b, carry):
        base = b * 128
        sel = onehot(iota((128, 256), 0) + base == place)
        extra = onehot(iota((128, 128), 0) + base == iota((128, 128), 1) * 8 + 6)
        out = dot(sel, mfeat_ref[...]) + dot(extra, tags)
        msg[pl.ds(b * 16, 16)] = jnp.concatenate(
            [out[:, :128].reshape(16, 8, 128), out[:, 128:].reshape(16, 8, 128)], axis=1
        ).astype(bf16)
        return carry

    lax.fori_loop(0, 8, pack, 0)

    crep = jnp.broadcast_to(coef_ref[...], (128, coef_ref.shape[1])).astype(bf16)
    eye = iota((128, 128), 0) == iota((128, 128), 1)
    for c in range(chunks):
        feature_copy(c).wait()
        out = dot_nt(fbuf[c * rows_chunk : (c + 1) * rows_chunk, :], crep)
        lines = jnp.sum(jnp.where(eye, out.reshape(rows_chunk // 128, 128, 128), 0.0), axis=1)
        for j in range(rows_chunk // 256):
            part[c * (rows_chunk // 256) + j] = lines[2 * j : 2 * j + 2]

    pl.semaphore_wait(barrier, n_dev - 1)

    def send_part(d):
        f = lax.rem(feat + d, n_feat)
        send(part.at[f], rs.at[feat], 0, (dp, f)).start()

    others(n_feat, send_part)

    def send_rows(d):
        t = lax.rem(me + d, n_dev)
        send(msg.at[t], rin.at[me], 1, device(t)).start()

    others(n_dev, send_rows)
    rs[feat] = part[feat]
    rin[me] = msg[me]

    arrived(rs.at[pl.ds(0, n_feat - 1)], 0)
    score = rs[0]
    for f in range(1, n_feat):
        score = score + rs[f]
    own[...] = score
    ag[feat] = score
    own_row = two_rows(score)
    lane_hot = iota((128, 256), 0) == lane_of[...]
    parts = [
        dot_nt(owner_hot[...], jnp.where(lane_hot, t.astype(f32), 0.0).astype(bf16))
        for t in split3(own_row)
    ]
    by = (parts[0] + parts[1]) + parts[2]
    sc[...] = by.reshape(n_dev, 1, 128)

    def send_score(d):
        t = lax.rem(me + d, n_dev)
        send(sc.at[t], scr.at[me], 2, device(t)).start()

    others(n_dev, send_score)

    def send_own(d):
        f = lax.rem(feat + d, n_feat)
        send(own, ag.at[feat], 3, (dp, f)).start()

    others(n_feat, send_own)
    scr[me] = sc[me]

    arrived(rin.at[pl.ds(0, n_dev - 1)], 1)

    def unpack(b, carry):
        got = rin[pl.ds(b * 16, 16)].astype(f32)
        rows_src[pl.ds(b * 128, 128), :] = jnp.concatenate(
            [got[:, 0:8].reshape(128, 128), got[:, 8:16].reshape(128, 128)], axis=1
        ).astype(bf16)
        return carry

    lax.fori_loop(0, 8, unpack, 0)
    src = iota((8, 1024), 1)
    tag_sel = onehot(((src & 7) == 6) & ((src >> 7) == iota((8, 1024), 0)))
    tags_in = dot(tag_sel, rows_src[...])
    tag_in = (tags_in[:, :128] * 32.0 + tags_in[:, 128:]).astype(i32) - 1
    used = tag_in >= 0
    slot_in = jnp.where(used, tag_in >> 1, -1)
    label_in = jnp.where(used, tag_in & 1, 0)

    def line(x):
        return jnp.concatenate([x[a : a + 1] for a in range(8)], axis=1)

    slot_line = line(slot_in)
    member_line = slot_line >> 6
    spot_line = jnp.where(slot_line < 0, -1, slot_line & 63)
    mine = iota((8, 1024), 0) == member_line
    bhot[...] = onehot((iota((128, 1024), 0) & 63) == spot_line)

    for h in range(4):
        sel = onehot(iota((128, 1024), 0) + 128 * h == slot_line)
        padded[128 * h : 128 * h + 128, :] = dot(sel, rows_src[...]).astype(bf16)

    low = iota((32, 128), 1) < 64
    for h in range(4):
        pair = padded[128 * h : 128 * h + 128, :]
        prod = dot_nt(pair, pair)
        turned = pltpu.roll(prod, 64, 1)
        gram[pl.ds(2 * h, 32, stride=8), :] = jnp.where(low, prod[0:32], turned[32:64])
        gram[pl.ds(2 * h + 1, 32, stride=8), :] = jnp.where(low, turned[64:96], prod[96:128])

    marks = jnp.concatenate(
        [jnp.where(mine, line(label_in).astype(f32), 0.0), jnp.where(mine, 1.0, 0.0)], axis=0
    ).astype(bf16)
    marked = dot_nt(marks, bhot[...])
    label, live = marked[0:8], marked[8:16]

    member_of = iota((8, 512), 1) >> 6 == iota((8, 512), 0)
    first = jnp.where(member_of, fold3(dot_nt(stack3(mcoef_ref[...]), padded[...])), 0.0)
    first = (first[:, 0:128] + first[:, 128:256]) + (first[:, 256:384] + first[:, 384:512])
    start = first + pltpu.roll(first, 64, 1)

    arrived(ag.at[pl.ds(0, n_feat - 1)], 3)
    scores = jnp.concatenate([ag[f] for f in range(n_feat)], axis=0)
    resid = jax.nn.sigmoid(scores + mscore_ref[...]) - click_ref[...].astype(f32)
    grad = jnp.zeros((8, grad_ref.shape[1]), f32)
    for b in range(4):
        eight = resid[8 * b : 8 * b + 8]
        wide = jnp.concatenate([eight] * 8, axis=1)
        wide = jnp.where(iota((8, 1024), 1) >> 7 == iota((8, 1024), 0), wide, 0.0).astype(bf16)
        grad = grad + dot(wide, fbuf[1024 * b : 1024 * b + 1024, :])
    gsrc[...] = jnp.sum(grad, axis=0, keepdims=True)

    def send_grad(d):
        t = lax.rem(dp + d, n_dp)
        send(gsrc, gin.at[dp], 4, (t, feat)).start()

    others(n_dp, send_grad)
    gin[dp] = gsrc[...]

    arrived(scr.at[pl.ds(0, n_dev - 1)], 2)
    score_in = [jnp.sum(scr[16 * a : 16 * a + 16], axis=0) for a in range(8)]
    score_line = jnp.concatenate(score_in, axis=1)
    offset = fold3(dot_nt(stack3(jnp.where(mine, score_line, 0.0)), bhot[...]))

    lane = iota((8, 128), 1)
    low = lane < 64

    def newton(step, carry):
        u, _ = carry
        prob = jax.nn.sigmoid(offset + u)
        slope = live * (prob - label)
        root = jnp.sqrt(live * prob * (1.0 - prob))
        rhs = root * (gram_times(gram, slope) + u)
        rows = []
        for p in range(32):
            scaled = gram[8 * p : 8 * p + 8, :] * root * take(root, jnp.where(low, p, p + 32))
            diagonal = (lane == p) | (lane == p + 96)
            rows.append(scaled + jnp.where(diagonal, 1.0, 0.0))
        beta = root * solve(rows, rhs) - slope
        return gram_times(gram, beta), beta

    value, beta = lax.fori_loop(0, NEWTON, newton, (start, jnp.zeros((8, 128), f32)))

    back = fold3(dot(stack3(jnp.where(low, value, 0.0)), bhot[...]))
    back = jnp.sum(jnp.where(mine, back, 0.0), axis=0, keepdims=True)
    for a in range(8):
        bk[a] = back[:, 128 * a : 128 * a + 128]

    def send_back(d):
        t = lax.rem(me + d, n_dev)
        send(bk.at[t // n_feat], ret.at[me], 5, device(t)).start()

    others(n_dev, send_back)
    ret[me] = bk[dp]

    spread = jnp.where(member_of, jnp.concatenate([beta] * 4, axis=1), 0.0)
    coefs_ref[...] = fold3(dot(stack3(spread), padded[...]))

    arrived(gin.at[pl.ds(0, n_dp - 1)], 4)
    full = gin[0]
    for t in range(1, n_dp):
        full = full + gin[t]
    grad_ref[...] = full / math.sqrt(n_dev * 256)

    sent(part.at[pl.ds(0, n_feat - 1)], 0)
    sent(msg.at[pl.ds(0, n_dev - 1)], 1)
    sent(sc.at[pl.ds(0, n_dev - 1)], 2)
    sent(ag.at[pl.ds(0, n_feat - 1)], 3)
    sent(gin.at[pl.ds(0, n_dp - 1)], 4)

    arrived(ret.at[pl.ds(0, n_dev - 1)], 5)
    lane_half = onehot(iota((128, 256), 0) == lane_of[...])
    came = ret[...].reshape(n_dev, 128)
    got = [dot(t, lane_half) for t in split3(came)]
    got = (got[0] + got[1]) + got[2]
    mine_back = jnp.sum(jnp.where(iota((n_dev, 256), 0) == slot_ref[...] >> 9, got, 0.0), axis=0)
    total_ref[...] = two_rows(own[...]) + mine_back[None, :]
    sent(ret.at[pl.ds(0, n_dev - 1)], 5)


def per_device(
    features, fixed_coef, member_score, clicks, member_features, member_coef, block_slot
):
    n_dev = 128
    rows, width = features.shape
    vmem = pl.BlockSpec(memory_space=pltpu.VMEM)
    grad, coefs, total = pl.pallas_call(
        kernel,
        name="glmix",
        out_shape=(
            jax.ShapeDtypeStruct((1, width), f32),
            jax.ShapeDtypeStruct(member_coef.shape, f32),
            jax.ShapeDtypeStruct((1, block_slot.shape[0]), f32),
        ),
        in_specs=[vmem] * 6 + [pl.BlockSpec(memory_space=pl.ANY)],
        out_specs=(vmem,) * 3,
        scratch_shapes=[
            pltpu.VMEM((rows, width), bf16),
            pltpu.VMEM((n_dev, 16, 128), bf16),
            pltpu.VMEM((n_dev, 16, 128), bf16),
            pltpu.VMEM((16, 2, 128), f32),
            pltpu.VMEM((16, 2, 128), f32),
            pltpu.VMEM((2, 128), f32),
            pltpu.VMEM((16, 2, 128), f32),
            pltpu.VMEM((n_dev, 1, 128), f32),
            pltpu.VMEM((n_dev, 1, 128), f32),
            pltpu.VMEM((8, 1, 128), f32),
            pltpu.VMEM((n_dev, 1, 128), f32),
            pltpu.VMEM((1, width), f32),
            pltpu.VMEM((8, 1, width), f32),
            pltpu.VMEM((n_dev, 256), bf16),
            pltpu.VMEM((1, 256), i32),
            pltpu.VMEM((1024, 256), bf16),
            pltpu.VMEM((128, 1024), bf16),
            pltpu.VMEM((512, 256), bf16),
            pltpu.VMEM((256, 128), f32),
            pltpu.SemaphoreType.DMA((8,)),
            pltpu.SemaphoreType.DMA((6,)),
            pltpu.SemaphoreType.DMA((6,)),
        ],
        compiler_params=pltpu.CompilerParams(collective_id=0, has_side_effects=True),
    )(
        fixed_coef.reshape(1, width),
        member_score.reshape(rows // 128, 128),
        clicks.reshape(rows // 128, 128),
        member_features,
        member_coef,
        block_slot.reshape(1, -1),
        features,
    )
    return grad.reshape(-1), coefs, total.reshape(-1)


def solution(mesh):
    return jax.shard_map(
        per_device,
        mesh=mesh,
        in_specs=(
            P("dp", "feat"),
            P("feat"),
            P("dp"),
            P("dp"),
            P(("dp", "feat"), None),
            P(("dp", "feat"), None),
            P(("dp", "feat")),
        ),
        out_specs=(P("feat"), P(("dp", "feat"), None), P(("dp", "feat"))),
        check_vma=False,
    )
```

time: 236 us -> 50.4 us (0.21)
  blocking collectives: 75.1 us -> 0 us
  matrix products: 70.7 us -> 0 us
  Pallas kernels: 0 us -> 45.8 us
  starting transfers between devices: 35.3 us -> 0 us
  local copies, waits for them, and re-layouts: 32.6 us -> 3.76 us
  waiting for transfers between devices: 12.6 us -> 0 us
  other arithmetic: 5.86 us -> 0 us
    psum x2 -> x0, blocking collectives: 75.1 us -> none  [the longest x1 62.3 us: per_device(): fixed_score = lax.psum(partial_score, 'feat')]
    dot_general x139 -> x0, matrix products: 70.7 us -> none  [the longest x60 32.8 us: sweep(): product = jnp.einsum('mbc,mcd->mbd', system, approx, precision=high)]
    pallas_call x0 -> x1, Pallas kernels: none -> 45.8 us  [per_device(): pl.pallas_call(kernel, name='glmix', out_shape=(jax.ShapeDtypeStruct((1,...]
    all_to_all x3 -> x0, starting transfers between devices: 35.3 us -> none  [the longest x1 18.9 us: per_device(): lax.all_to_all(meta_out.reshape(2, devices, capacity), ('dp', 'feat'), sp...]
    scatter x7 -> x0, local copies, waits for them, and re-layouts: 20.7 us -> none  [the longest x1 5.62 us: per_device(): padded_rows = jnp.zeros((slot_count + 1, width), jnp.float32).at[where_lo...]
    all_to_all x3 -> x0, waiting for transfers between devices: 12.6 us -> none  [the longest x1 9.8 us: per_device(): lax.all_to_all(back_value.reshape(devices, capacity), ('dp', 'feat'), spl...]
    gather x3 -> x0, local copies, waits for them, and re-layouts: 6.51 us -> none  [the longest x2 5.14 us: per_device(): member_value[jnp.minimum(where_local, slot_count - 1)]]
    unnamed x9 -> x3, local copies, waits for them, and re-layouts: 0.03 us -> 3.76 us
  transfers between devices with their start and end apart: 3 -> 0, of which waited for: 2 -> 0; matrix products, arithmetic and copies ran while one was open for 7% -> 0% of each run, Pallas kernels for 0% -> 0%
where the time goes in v1:
time: 50.4 us; the launch traced here: 50.2 us
  Pallas kernels  45.8 us (91%)
  local copies, waits for them, and re-layouts  3.76 us (7%)
  between operations  0.64 us (1%)
    pallas_call x1, Pallas kernels, per_device(): pl.pallas_call(kernel, name='glmix', out_shape=(jax.ShapeDtypeStruct((1,...  45.8 us
    unnamed x3, local copies, waits for them, and re-layouts  3.76 us

profile of v1, /device:TPU:1, one launch (start us, length us, event | category | flops | bytes accessed | tf_op | source)
XLA Modules:
  0.0 50.2 jit_solution(9537624893012898227)
XLA Ops:
  0.6 45.8 %glmix.1 = (f32[1,512]{1,0:T(1,128)}, f32[8,256]{1,0:T(8,128)}, f32[1,256]{1,0:T(1,128)}) custom-call(f32[1,512]{1,0:T(1,128)} %bitcast.8, f32[32,128]{1,0:T(8,128)} %bitcast.6, s32[32,128]{1,0:T(8,128)} %bitcast.7, bf16[256,256]{1,0:T(8,128)(2,1)} %mfeat_ref.1, f32[8,256]{1,0:T(8,128)} %mcoef_ref.1, s32[1,256]{1,0:T(1,128)} %bitcast.10, ...), custom_call_target="tpu_custom_call" | custom-call | tf_op jit(solution)/shard_map/glmix/pallas_call | solution.py:396
  46.5 1.2 %copy.13 = f32[512]{0:T(512)} copy(f32[512]{0:T(512)} %bitcast.9) | data formatting | bytes 4096
  47.7 1.3 %copy.14 = f32[8,256]{1,0:T(8,128)} copy(f32[8,256]{1,0:T(8,128)} %get-tuple-element.13) | data formatting | bytes 16384
  49.0 1.2 %copy.15 = f32[256]{0:T(256)} copy(f32[256]{0:T(256)} %bitcast.11) | data formatting | bytes 2048

commit v2 on v1

--- a/solution.py
+++ b/solution.py
@@ -7,7 +7,8 @@
 from jax.experimental.pallas import tpu as pltpu
 from jax.sharding import PartitionSpec as P
 
-MESH = pl.DeviceIdType.MESH
+SPLIT = 84
+LOGICAL = pl.DeviceIdType.LOGICAL
 BLK = 64
 NEWTON = 3
 PAIRS = 4
@@ -120,11 +121,12 @@
 
 
 def kernel(
-    coef_ref, mscore_ref, click_ref, mfeat_ref, mcoef_ref, slot_ref, feat_ref,
-    grad_ref, coefs_ref, total_ref,
+    coef_hbm, mscore_hbm, click_hbm, mfeat_hbm, mcoef_hbm, slot_hbm, feat_ref,
+    out_ref,
+    coef_ref, mscore_ref, click_ref, mfeat_ref, mcoef_ref, slot_ref,
     fbuf, msg, rin, part, rs, own, ag, sc, scr, bk, ret, gsrc, gin,
     owner_hot, lane_of, rows_src, bhot, padded, gram,
-    fsem, ssem, rsem,
+    isem, fsem, ssem, rsem,
 ):
     n_dp, n_feat = 8, 16
     n_dev = n_dp * n_feat
@@ -138,39 +140,51 @@
         window = pl.ds(c * rows_chunk, rows_chunk)
         return pltpu.make_async_copy(feat_ref.at[window], fbuf.at[window], fsem.at[c])
 
+    loads = [
+        pltpu.make_async_copy(src, dst, isem.at[i])
+        for i, (src, dst) in enumerate([
+            (slot_hbm, slot_ref), (click_hbm, click_ref), (mfeat_hbm, mfeat_ref),
+            (coef_hbm, coef_ref), (mscore_hbm, mscore_ref), (mcoef_hbm, mcoef_ref),
+        ])
+    ]
+    for load in loads:
+        load.start()
     for c in range(chunks):
         feature_copy(c).start()
 
     barrier = pltpu.get_barrier_semaphore()
 
-    def device(t):
-        return (t // n_feat, lax.rem(t, n_feat))
-
-    def others(n, body):
-        def step(d, carry):
-            body(d)
-            return carry
-
-        lax.fori_loop(1, n, step, 0)
-
-    def hello(d):
-        t = lax.rem(me + d, n_dev)
-        pl.semaphore_signal(barrier, inc=1, device_id=device(t), device_id_type=MESH)
-
-    others(n_dev, hello)
+    dps = [2 * lax.rem(dp // 2 + dy, 4) + lax.rem(dp + dc, 2) for dy in range(4) for dc in range(2)]
+    feats = [
+        4 * lax.rem(feat // 4 + dz, 4) + lax.rem(feat + dx, 4) for dz in range(4) for dx in range(4)
+    ]
+    hops = [0, 1, 2, 1]
+    dp_far = sorted(range(1, 8), key=lambda a: -hops[a // 2])
+    feat_far = sorted(range(1, 16), key=lambda b: -hops[b // 4] - hops[b % 4])
+    all_far = sorted(
+        ((a, b) for a in range(8) for b in range(16) if a or b),
+        key=lambda ab: -hops[ab[0] // 2] - hops[ab[1] // 4] - hops[ab[1] % 4],
+    )
+
+    for a, b in all_far:
+        pl.semaphore_signal(
+            barrier, inc=1, device_id=dps[a] * n_feat + feats[b], device_id_type=LOGICAL
+        )
 
     def send(src, dst, which, target):
         return pltpu.make_async_remote_copy(
             src_ref=src, dst_ref=dst, send_sem=ssem.at[which], recv_sem=rsem.at[which],
-            device_id=target, device_id_type=MESH,
+            device_id=target, device_id_type=LOGICAL,
         )
 
     def arrived(ref, which):
-        send(ref, ref, which, (dp, feat)).wait_recv()
+        send(ref, ref, which, me).wait_recv()
 
     def sent(ref, which):
-        send(ref, ref, which, (dp, feat)).wait_send()
-
+        send(ref, ref, which, me).wait_send()
+
+    for load in loads:
+        load.wait()
     slots = slot_ref[...]
     owner = slots >> 9
     own_clicks = two_rows(click_ref[pl.ds(2 * feat, 2), :])
@@ -205,28 +219,22 @@
 
     lax.fori_loop(0, 8, pack, 0)
 
-    crep = jnp.broadcast_to(coef_ref[...], (128, coef_ref.shape[1])).astype(bf16)
-    eye = iota((128, 128), 0) == iota((128, 128), 1)
+    coef = jnp.broadcast_to(coef_ref[...], (8, coef_ref.shape[1])).astype(bf16)
     for c in range(chunks):
         feature_copy(c).wait()
-        out = dot_nt(fbuf[c * rows_chunk : (c + 1) * rows_chunk, :], crep)
-        lines = jnp.sum(jnp.where(eye, out.reshape(rows_chunk // 128, 128, 128), 0.0), axis=1)
+        out = dot_nt(coef, fbuf[c * rows_chunk : (c + 1) * rows_chunk, :])[0:1]
         for j in range(rows_chunk // 256):
-            part[c * (rows_chunk // 256) + j] = lines[2 * j : 2 * j + 2]
+            part[c * (rows_chunk // 256) + j] = out[:, 256 * j : 256 * j + 256]
 
     pl.semaphore_wait(barrier, n_dev - 1)
 
-    def send_part(d):
-        f = lax.rem(feat + d, n_feat)
-        send(part.at[f], rs.at[feat], 0, (dp, f)).start()
-
-    others(n_feat, send_part)
-
-    def send_rows(d):
-        t = lax.rem(me + d, n_dev)
-        send(msg.at[t], rin.at[me], 1, device(t)).start()
-
-    others(n_dev, send_rows)
+    for b in feat_far:
+        send(part.at[feats[b]], rs.at[feat], 0, dp * n_feat + feats[b]).start()
+
+    for a, b in all_far[:SPLIT]:
+        t = dps[a] * n_feat + feats[b]
+        send(msg.at[t], rin.at[me], 1, t).start()
+
     rs[feat] = part[feat]
     rin[me] = msg[me]
 
@@ -236,26 +244,25 @@
         score = score + rs[f]
     own[...] = score
     ag[feat] = score
-    own_row = two_rows(score)
     lane_hot = iota((128, 256), 0) == lane_of[...]
     parts = [
         dot_nt(owner_hot[...], jnp.where(lane_hot, t.astype(f32), 0.0).astype(bf16))
-        for t in split3(own_row)
+        for t in split3(score)
     ]
     by = (parts[0] + parts[1]) + parts[2]
     sc[...] = by.reshape(n_dev, 1, 128)
 
-    def send_score(d):
-        t = lax.rem(me + d, n_dev)
-        send(sc.at[t], scr.at[me], 2, device(t)).start()
-
-    others(n_dev, send_score)
-
-    def send_own(d):
-        f = lax.rem(feat + d, n_feat)
-        send(own, ag.at[feat], 3, (dp, f)).start()
-
-    others(n_feat, send_own)
+    for a, b in all_far:
+        t = dps[a] * n_feat + feats[b]
+        send(sc.at[t], scr.at[me], 2, t).start()
+
+    for a, b in all_far[SPLIT:]:
+        t = dps[a] * n_feat + feats[b]
+        send(msg.at[t], rin.at[me], 1, t).start()
+
+    for b in feat_far:
+        send(own, ag.at[feat], 3, dp * n_feat + feats[b]).start()
+
     scr[me] = sc[me]
 
     arrived(rin.at[pl.ds(0, n_dev - 1)], 1)
@@ -307,24 +314,6 @@
     first = jnp.where(member_of, fold3(dot_nt(stack3(mcoef_ref[...]), padded[...])), 0.0)
     first = (first[:, 0:128] + first[:, 128:256]) + (first[:, 256:384] + first[:, 384:512])
     start = first + pltpu.roll(first, 64, 1)
-
-    arrived(ag.at[pl.ds(0, n_feat - 1)], 3)
-    scores = jnp.concatenate([ag[f] for f in range(n_feat)], axis=0)
-    resid = jax.nn.sigmoid(scores + mscore_ref[...]) - click_ref[...].astype(f32)
-    grad = jnp.zeros((8, grad_ref.shape[1]), f32)
-    for b in range(4):
-        eight = resid[8 * b : 8 * b + 8]
-        wide = jnp.concatenate([eight] * 8, axis=1)
-        wide = jnp.where(iota((8, 1024), 1) >> 7 == iota((8, 1024), 0), wide, 0.0).astype(bf16)
-        grad = grad + dot(wide, fbuf[1024 * b : 1024 * b + 1024, :])
-    gsrc[...] = jnp.sum(grad, axis=0, keepdims=True)
-
-    def send_grad(d):
-        t = lax.rem(dp + d, n_dp)
-        send(gsrc, gin.at[dp], 4, (t, feat)).start()
-
-    others(n_dp, send_grad)
-    gin[dp] = gsrc[...]
 
     arrived(scr.at[pl.ds(0, n_dev - 1)], 2)
     score_in = [jnp.sum(scr[16 * a : 16 * a + 16], axis=0) for a in range(8)]
@@ -355,21 +344,39 @@
     for a in range(8):
         bk[a] = back[:, 128 * a : 128 * a + 128]
 
-    def send_back(d):
-        t = lax.rem(me + d, n_dev)
-        send(bk.at[t // n_feat], ret.at[me], 5, device(t)).start()
-
-    others(n_dev, send_back)
+    for a, b in all_far:
+        send(bk.at[dps[a]], ret.at[me], 5, dps[a] * n_feat + feats[b]).start()
+
     ret[me] = bk[dp]
 
+    arrived(ag.at[pl.ds(0, n_feat - 1)], 3)
+    scores = jnp.concatenate(
+        [ag[f][:, 128 * h : 128 * h + 128] for f in range(n_feat) for h in range(2)], axis=0
+    )
+    resid = jax.nn.sigmoid(scores + mscore_ref[...]) - click_ref[...].astype(f32)
+    grad = jnp.zeros((8, fbuf.shape[1]), f32)
+    for b in range(4):
+        eight = resid[8 * b : 8 * b + 8]
+        wide = jnp.concatenate([eight] * 8, axis=1)
+        wide = jnp.where(iota((8, 1024), 1) >> 7 == iota((8, 1024), 0), wide, 0.0).astype(bf16)
+        grad = grad + dot(wide, fbuf[1024 * b : 1024 * b + 1024, :])
+    gsrc[...] = jnp.sum(grad, axis=0, keepdims=True)
+
+    for a in dp_far:
+        send(gsrc, gin.at[dp], 4, dps[a] * n_feat + feat).start()
+
+    gin[dp] = gsrc[...]
+
     spread = jnp.where(member_of, jnp.concatenate([beta] * 4, axis=1), 0.0)
-    coefs_ref[...] = fold3(dot(stack3(spread), padded[...]))
+    out_ref[0:8, :] = fold3(dot(stack3(spread), padded[...]))
 
     arrived(gin.at[pl.ds(0, n_dp - 1)], 4)
     full = gin[0]
     for t in range(1, n_dp):
         full = full + gin[t]
-    grad_ref[...] = full / math.sqrt(n_dev * 256)
+    full = full / math.sqrt(n_dev * 256)
+    out_ref[8:9, :] = full[:, :256]
+    out_ref[9:10, :] = full[:, 256:]
 
     sent(part.at[pl.ds(0, n_feat - 1)], 0)
     sent(msg.at[pl.ds(0, n_dev - 1)], 1)
@@ -383,8 +390,14 @@
     got = [dot(t, lane_half) for t in split3(came)]
     got = (got[0] + got[1]) + got[2]
     mine_back = jnp.sum(jnp.where(iota((n_dev, 256), 0) == slot_ref[...] >> 9, got, 0.0), axis=0)
-    total_ref[...] = two_rows(own[...]) + mine_back[None, :]
+    out_ref[10:11, :] = own[...] + mine_back[None, :]
     sent(ret.at[pl.ds(0, n_dev - 1)], 5)
+
+
+def split(merged_ref, grad_ref, coefs_ref, total_ref):
+    coefs_ref[...] = merged_ref[0:8, :]
+    grad_ref[...] = jnp.concatenate([merged_ref[8:9, :], merged_ref[9:10, :]], axis=1)
+    total_ref[...] = merged_ref[10:11, :]
 
 
 def per_device(
@@ -393,24 +406,26 @@
     n_dev = 128
     rows, width = features.shape
     vmem = pl.BlockSpec(memory_space=pltpu.VMEM)
-    grad, coefs, total = pl.pallas_call(
+    merged = pl.pallas_call(
         kernel,
         name="glmix",
-        out_shape=(
-            jax.ShapeDtypeStruct((1, width), f32),
-            jax.ShapeDtypeStruct(member_coef.shape, f32),
-            jax.ShapeDtypeStruct((1, block_slot.shape[0]), f32),
-        ),
-        in_specs=[vmem] * 6 + [pl.BlockSpec(memory_space=pl.ANY)],
-        out_specs=(vmem,) * 3,
+        out_shape=jax.ShapeDtypeStruct((16, 256), f32),
+        in_specs=[pl.BlockSpec(memory_space=pl.ANY)] * 7,
+        out_specs=vmem,
         scratch_shapes=[
+            pltpu.VMEM((1, width), f32),
+            pltpu.VMEM((rows // 128, 128), f32),
+            pltpu.VMEM((rows // 128, 128), i32),
+            pltpu.VMEM(member_features.shape, bf16),
+            pltpu.VMEM(member_coef.shape, f32),
+            pltpu.VMEM((1, 256), i32),
             pltpu.VMEM((rows, width), bf16),
             pltpu.VMEM((n_dev, 16, 128), bf16),
             pltpu.VMEM((n_dev, 16, 128), bf16),
-            pltpu.VMEM((16, 2, 128), f32),
-            pltpu.VMEM((16, 2, 128), f32),
-            pltpu.VMEM((2, 128), f32),
-            pltpu.VMEM((16, 2, 128), f32),
+            pltpu.VMEM((16, 1, 256), f32),
+            pltpu.VMEM((16, 1, 256), f32),
+            pltpu.VMEM((1, 256), f32),
+            pltpu.VMEM((16, 1, 256), f32),
             pltpu.VMEM((n_dev, 1, 128), f32),
             pltpu.VMEM((n_dev, 1, 128), f32),
             pltpu.VMEM((8, 1, 128), f32),
@@ -423,6 +438,7 @@
             pltpu.VMEM((128, 1024), bf16),
             pltpu.VMEM((512, 256), bf16),
             pltpu.VMEM((256, 128), f32),
+            pltpu.SemaphoreType.DMA((6,)),
             pltpu.SemaphoreType.DMA((8,)),
             pltpu.SemaphoreType.DMA((6,)),
             pltpu.SemaphoreType.DMA((6,)),
@@ -437,6 +453,17 @@
         block_slot.reshape(1, -1),
         features,
     )
+    grad, coefs, total = pl.pallas_call(
+        split,
+        name="split",
+        out_shape=(
+            jax.ShapeDtypeStruct((1, width), f32),
+            jax.ShapeDtypeStruct(member_coef.shape, f32),
+            jax.ShapeDtypeStruct((1, block_slot.shape[0]), f32),
+        ),
+        in_specs=[vmem],
+        out_specs=(vmem,) * 3,
+    )(merged)
     return grad.reshape(-1), coefs, total.reshape(-1)
 
 

time: 50.4 us -> 42.2 us (0.84)
  Pallas kernels: 45.8 us -> 41.4 us
  local copies, waits for them, and re-layouts: 3.76 us -> 0 us
    pallas_call x1 -> x2, Pallas kernels: 45.8 us -> 41.4 us  [the longest x1 40.1 us: per_device(): pl.pallas_call(kernel, name='glmix', out_shape=jax.ShapeDtypeStruct((16,...]
    unnamed x3 -> x0, local copies, waits for them, and re-layouts: 3.76 us -> none
where the time goes in v2:
time: 42.2 us; the launch traced here: 42.1 us
  Pallas kernels  41.4 us (98%)
  between operations  0.64 us (2%)
    pallas_call x1, Pallas kernels, per_device(): pl.pallas_call(kernel, name='glmix', out_shape=jax.ShapeDtypeStruct((16,...  40.1 us
    pallas_call x1, Pallas kernels, per_device(): pl.pallas_call(split, name='split', out_shape=(jax.ShapeDtypeStruct((1, w...  1.32 us

profile of v2, /device:TPU:1, one launch (start us, length us, event | category | flops | bytes accessed | tf_op | source)
XLA Modules:
  0.0 42.1 jit_solution(15540885456656239012)
XLA Ops:
  0.6 40.1 %glmix.1.merged_ref = f32[16,256]{1,0:T(8,128)} custom-call(f32[1,512]{1,0:T(1,128)} %bitcast.8, f32[32,128]{1,0:T(8,128)} %bitcast.6, s32[32,128]{1,0:T(8,128)} %bitcast.7, bf16[256,256]{1,0:T(8,128)(2,1)} %mfeat_hbm.1, f32[8,256]{1,0:T(8,128)} %mcoef_hbm.1, s32[1,256]{1,0:T(1,128)} %bitcast.9, bf16[4096,512]{1,0:T(8,128)(2,1)} %feat_ref.1), custom_call_target="tpu_custom_call" | custom-call | tf_op jit(solution)/shard_map/glmix/pallas_call | solution.py:409
  40.7 1.3 %split.1 = (f32[1,512]{1,0:T(1,128)}, f32[8,256]{1,0:T(8,128)}, f32[1,256]{1,0:T(1,128)}) custom-call(f32[16,256]{1,0:T(8,128)} %glmix.1.merged_ref), custom_call_target="tpu_custom_call" | custom-call | tf_op jit(solution)/shard_map/split/pallas_call | solution.py:456

commit v3 on v2

--- a/solution.py
+++ b/solution.py
@@ -60,63 +60,70 @@
     lane = iota((8, 128), 1)
     low = lane < 64
     col = lane & 63
+    half = lane & 31
     rows = list(rows)
     s = jnp.zeros((8, 128), f32)
     for q in range(0, 32, PAIRS):
-        raw, vars_, offs, pivots = [], [], [], []
-        for p in range(q, q + PAIRS):
-            rolled = pltpu.roll(rows[p], 64, 1)
-            raw += [rows[p], rows[p]]
-            offs += [0, 64]
-            vars_ += [p, p + 32]
-            pivots += [jnp.where(low, rows[p], rolled), jnp.where(low, rolled, rows[p])]
-        n = len(vars_)
-        block = {
-            (i, j): jnp.broadcast_to(
-                raw[i][:, offs[i] + vars_[j] : offs[i] + vars_[j] + 1], (8, 128)
-            )
-            for i in range(n)
-            for j in range(i, n)
-        }
-        ys = [jnp.broadcast_to(y[:, v : v + 1], (8, 128)) for v in vars_]
-        half = col & 31
+        unknowns = [b + p for b in (0, 32) for p in range(q, q + PAIRS)]
+        n = len(unknowns)
+        sides = [jnp.where(low, v, v + 64) for v in unknowns]
+        block = {}
+        for j, v in enumerate(unknowns):
+            for i in range(min(j + 1, PAIRS)):
+                block[i, j] = jnp.broadcast_to(rows[q + i][:, v : v + 1], (8, 128))
+            for i in range(PAIRS, j + 1):
+                block[i, j] = jnp.broadcast_to(rows[q + i - PAIRS][:, v + 64 : v + 65], (8, 128))
+        ys = [jnp.broadcast_to(y[:, v : v + 1], (8, 128)) for v in unknowns]
+        rolled = [pltpu.roll(rows[p], 64, 1) for p in range(q, q + PAIRS)]
+        pivots = [jnp.where(low, rows[q + i], rolled[i]) for i in range(PAIRS)]
+        pivots += [jnp.where(low, rolled[i], rows[q + i]) for i in range(PAIRS)]
         inside = (half >= q) & (half < q + PAIRS)
         done = half < q + PAIRS
         t = [
-            jnp.where(col == vars_[i], 1.0, jnp.where(inside, 0.0, pivots[i])) for i in range(n)
+            jnp.where(col == unknowns[i], 1.0, jnp.where(inside, 0.0, pivots[i])) for i in range(n)
         ]
-        inv, factor = [], {}
-        for k in range(n):
-            inv.append(1.0 / block[k, k])
-            for i in range(k + 1, n):
-                factor[i, k] = block[k, i] * inv[k]
-            for i in range(k + 1, n):
-                t[i] = t[i] - factor[i, k] * t[k]
+        invs, factor = {}, {}
+        for k in range(0, n, 2):
+            a, b, c = block[k, k], block[k, k + 1], block[k + 1, k + 1]
+            scale = 1.0 / (a * c - b * b)
+            invs[k] = (c * scale, b * scale, a * scale)
+            for i in range(k + 2, n):
+                factor[i, k] = (c * block[k, i] - b * block[k + 1, i]) * scale
+                factor[i, k + 1] = (a * block[k + 1, i] - b * block[k, i]) * scale
+            for i in range(k + 2, n):
+                t[i] = t[i] - (factor[i, k] * t[k] + factor[i, k + 1] * t[k + 1])
                 for j in range(i, n):
-                    block[i, j] = block[i, j] - factor[i, k] * block[k, j]
-        t = [t[i] * inv[i] for i in range(n)]
-        for k in range(n - 1, 0, -1):
+                    block[i, j] = block[i, j] - (
+                        factor[i, k] * block[k, j] + factor[i, k + 1] * block[k + 1, j]
+                    )
+        for k in range(0, n, 2):
+            a, b, c = invs[k]
+            t[k], t[k + 1] = a * t[k] - b * t[k + 1], c * t[k + 1] - b * t[k]
+        for k in range(n - 2, 0, -2):
             for i in range(k):
-                t[i] = t[i] - factor[k, i] * t[k]
-        step = ys[0] * t[0]
-        for i in range(1, n):
-            step = step + ys[i] * t[i]
+                t[i] = t[i] - (factor[k, i] * t[k] + factor[k + 1, i] * t[k + 1])
+        step = tree_sum([ys[i] * t[i] for i in range(n)])
         s = s + jnp.where(done, step, 0.0)
         y = y - jnp.where(done, 0.0, step)
-        for p in range(q + PAIRS, 32):
-            pick = [jnp.where(low, off + p, off + p + 32) for off in (0, 64)]
-            new = jnp.where(inside, 0.0, rows[p])
-            for i in range(n):
-                new = new - take(raw[i], pick[i % 2]) * t[i]
-            rows[p] = new
+        for group in (range(q + PAIRS, min(q + 2 * PAIRS, 32)), range(q + 2 * PAIRS, 32)):
+            terms = [[take(rows[p], sides[i]) * t[i] for p in group] for i in range(n)]
+            for j, p in enumerate(group):
+                change = tree_sum([terms[i][j] for i in range(n)])
+                rows[p] = jnp.where(inside, 0.0, rows[p]) - change
     return s
+
+
+def tree_sum(terms):
+    while len(terms) > 1:
+        terms = [sum(terms[i + 1 : i + 2], terms[i]) for i in range(0, len(terms), 2)]
+    return terms[0]
 
 
 def gram_times(gram_ref, v):
     low = iota((8, 128), 1) < 64
-    total = jnp.zeros((8, 128), f32)
-    for p in range(32):
-        total = total + gram_ref[8 * p : 8 * p + 8, :] * take(v, jnp.where(low, p, p + 32))
+    total = tree_sum(
+        [gram_ref[8 * p : 8 * p + 8, :] * take(v, jnp.where(low, p, p + 32)) for p in range(32)]
+    )
     return total + pltpu.roll(total, 64, 1)
 
 
@@ -409,8 +416,8 @@
     merged = pl.pallas_call(
         kernel,
         name="glmix",
-        out_shape=jax.ShapeDtypeStruct((16, 256), f32),
-        in_specs=[pl.BlockSpec(memory_space=pl.ANY)] * 7,
+        out_shape=pltpu.VMEM((16, 256), f32),
+        in_specs=[pl.BlockSpec(memory_space=pltpu.HBM)] * 7,
         out_specs=vmem,
         scratch_shapes=[
             pltpu.VMEM((1, width), f32),
@@ -463,6 +470,7 @@
         ),
         in_specs=[vmem],
         out_specs=(vmem,) * 3,
+        compiler_params=pltpu.CompilerParams(vmem_limit_bytes=1 << 20),
     )(merged)
     return grad.reshape(-1), coefs, total.reshape(-1)
 

time: 42.2 us -> 38.3 us (0.908)
  Pallas kernels: 41.4 us -> 37.5 us
    pallas_call x1, Pallas kernels: 40.1 us -> 36.9 us  [per_device(): pl.pallas_call(kernel, name='glmix', out_shape=pltpu.VMEM((16, 256), f32)...]
    pallas_call x1, Pallas kernels: 1.32 us -> 0.6 us  [per_device(): pl.pallas_call(split, name='split', out_shape=(jax.ShapeDtypeStruct((1, w...]
where the time goes in v3:
time: 38.3 us; the launch traced here: 38.2 us
  Pallas kernels  37.5 us (98%)
  between operations  0.64 us (2%)
    pallas_call x1, Pallas kernels, per_device(): pl.pallas_call(kernel, name='glmix', out_shape=pltpu.VMEM((16, 256), f32)...  36.9 us

profile of v3, /device:TPU:1, one launch (start us, length us, event | category | flops | bytes accessed | tf_op | source)
XLA Modules:
  0.0 38.2 jit_solution(904176225598244742)
XLA Ops:
  0.6 36.9 %glmix.1.merged_ref = f32[16,256]{1,0:T(8,128)S(1)} custom-call(f32[1,512]{1,0:T(1,128)} %bitcast.8, f32[32,128]{1,0:T(8,128)} %bitcast.6, s32[32,128]{1,0:T(8,128)} %bitcast.7, bf16[256,256]{1,0:T(8,128)(2,1)} %mfeat_hbm.1, f32[8,256]{1,0:T(8,128)} %mcoef_hbm.1, s32[1,256]{1,0:T(1,128)} %bitcast.9, bf16[4096,512]{1,0:T(8,128)(2,1)} %feat_ref.1), custom_call_target="tpu_custom_call" | custom-call | tf_op jit(solution)/shard_map/glmix/pallas_call | solution.py:416
  37.6 0.6 %split.1 = (f32[1,512]{1,0:T(1,128)}, f32[8,256]{1,0:T(8,128)}, f32[1,256]{1,0:T(1,128)}) custom-call(f32[16,256]{1,0:T(8,128)S(1)} %glmix.1.merged_ref), custom_call_target="tpu_custom_call" | custom-call | tf_op jit(solution)/shard_map/split/pallas_call | solution.py:463

commit v4 on v3

--- a/solution.py
+++ b/solution.py
@@ -7,11 +7,11 @@
 from jax.experimental.pallas import tpu as pltpu
 from jax.sharding import PartitionSpec as P
 
-SPLIT = 84
+SPLIT = 104
 LOGICAL = pl.DeviceIdType.LOGICAL
 BLK = 64
 NEWTON = 3
-PAIRS = 4
+GROUPS = 2
 f32, bf16, i32 = jnp.float32, jnp.bfloat16, jnp.int32
 
 
@@ -58,30 +58,31 @@
 
 def solve(rows, y):
     lane = iota((8, 128), 1)
-    low = lane < 64
-    col = lane & 63
-    half = lane & 31
-    rows = list(rows)
-    s = jnp.zeros((8, 128), f32)
-    for q in range(0, 32, PAIRS):
-        unknowns = [b + p for b in (0, 32) for p in range(q, q + PAIRS)]
+    side = lane & 31
+    base = lane - side
+    group = lane & 15
+    rows = [list(pair) for pair in rows]
+    s = [jnp.zeros((8, 128), f32)] * 2
+    for q in range(0, 16, GROUPS):
+        unknowns = [16 * r + g for r in range(4) for g in range(q, q + GROUPS)]
         n = len(unknowns)
-        sides = [jnp.where(low, v, v + 64) for v in unknowns]
+
+        def at(x, place):
+            return jnp.broadcast_to(x[:, place : place + 1], (8, 128))
+
         block = {}
         for j, v in enumerate(unknowns):
-            for i in range(min(j + 1, PAIRS)):
-                block[i, j] = jnp.broadcast_to(rows[q + i][:, v : v + 1], (8, 128))
-            for i in range(PAIRS, j + 1):
-                block[i, j] = jnp.broadcast_to(rows[q + i - PAIRS][:, v + 64 : v + 65], (8, 128))
-        ys = [jnp.broadcast_to(y[:, v : v + 1], (8, 128)) for v in unknowns]
-        rolled = [pltpu.roll(rows[p], 64, 1) for p in range(q, q + PAIRS)]
-        pivots = [jnp.where(low, rows[q + i], rolled[i]) for i in range(PAIRS)]
-        pivots += [jnp.where(low, rolled[i], rows[q + i]) for i in range(PAIRS)]
-        inside = (half >= q) & (half < q + PAIRS)
-        done = half < q + PAIRS
-        t = [
-            jnp.where(col == unknowns[i], 1.0, jnp.where(inside, 0.0, pivots[i])) for i in range(n)
-        ]
+            for i, w in enumerate(unknowns[: j + 1]):
+                block[i, j] = at(rows[w % 16][v // 32], 32 * (w // 16) + v % 32)
+        ys = [at(y[v // 32], v % 32) for v in unknowns]
+        inside = (group >= q) & (group < q + GROUPS)
+        done = group < q + GROUPS
+        t = []
+        for v in unknowns:
+            own = [take(rows[v % 16][h], side + 32 * (v // 16)) for h in range(2)]
+            own = [jnp.where(inside, 0.0, x) for x in own]
+            own[v // 32] = jnp.where(side == v % 32, 1.0, own[v // 32])
+            t.append(own)
         invs, factor = {}, {}
         for k in range(0, n, 2):
             a, b, c = block[k, k], block[k, k + 1], block[k + 1, k + 1]
@@ -91,25 +92,36 @@
                 factor[i, k] = (c * block[k, i] - b * block[k + 1, i]) * scale
                 factor[i, k + 1] = (a * block[k + 1, i] - b * block[k, i]) * scale
             for i in range(k + 2, n):
-                t[i] = t[i] - (factor[i, k] * t[k] + factor[i, k + 1] * t[k + 1])
                 for j in range(i, n):
                     block[i, j] = block[i, j] - (
                         factor[i, k] * block[k, j] + factor[i, k + 1] * block[k + 1, j]
                     )
+                for h in range(2):
+                    t[i][h] = t[i][h] - (
+                        factor[i, k] * t[k][h] + factor[i, k + 1] * t[k + 1][h]
+                    )
         for k in range(0, n, 2):
             a, b, c = invs[k]
-            t[k], t[k + 1] = a * t[k] - b * t[k + 1], c * t[k + 1] - b * t[k]
+            for h in range(2):
+                t[k][h], t[k + 1][h] = (
+                    a * t[k][h] - b * t[k + 1][h],
+                    c * t[k + 1][h] - b * t[k][h],
+                )
         for k in range(n - 2, 0, -2):
             for i in range(k):
-                t[i] = t[i] - (factor[k, i] * t[k] + factor[k + 1, i] * t[k + 1])
-        step = tree_sum([ys[i] * t[i] for i in range(n)])
-        s = s + jnp.where(done, step, 0.0)
-        y = y - jnp.where(done, 0.0, step)
-        for group in (range(q + PAIRS, min(q + 2 * PAIRS, 32)), range(q + 2 * PAIRS, 32)):
-            terms = [[take(rows[p], sides[i]) * t[i] for p in group] for i in range(n)]
-            for j, p in enumerate(group):
-                change = tree_sum([terms[i][j] for i in range(n)])
-                rows[p] = jnp.where(inside, 0.0, rows[p]) - change
+                for h in range(2):
+                    t[i][h] = t[i][h] - (factor[k, i] * t[k][h] + factor[k + 1, i] * t[k + 1][h])
+        step = [tree_sum([ys[i] * t[i][h] for i in range(n)]) for h in range(2)]
+        s = [s[h] + jnp.where(done, step[h], 0.0) for h in range(2)]
+        y = [y[h] - jnp.where(done, 0.0, step[h]) for h in range(2)]
+        for part in (range(q + GROUPS, min(q + 2 * GROUPS, 16)), range(q + 2 * GROUPS, 16)):
+            picks = [
+                [take(rows[g][v // 32], base + v % 32) for g in part] for v in unknowns
+            ]
+            for at_, g in enumerate(part):
+                for h in range(2):
+                    change = tree_sum([picks[i][at_] * t[i][h] for i in range(n)])
+                    rows[g][h] = jnp.where(inside, 0.0, rows[g][h]) - change
     return s
 
 
@@ -119,12 +131,22 @@
     return terms[0]
 
 
+def by_rows(v, g):
+    lane = iota((8, 128), 1)
+    r = lane >> 5
+    return take(jnp.where(lane < 64, v[0], v[1]), 32 * r + 16 * (r & 1) + g)
+
+
 def gram_times(gram_ref, v):
-    low = iota((8, 128), 1) < 64
-    total = tree_sum(
-        [gram_ref[8 * p : 8 * p + 8, :] * take(v, jnp.where(low, p, p + 32)) for p in range(32)]
-    )
-    return total + pltpu.roll(total, 64, 1)
+    picks = [by_rows(v, g) for g in range(16)]
+    out = []
+    for h in range(2):
+        total = tree_sum(
+            [gram_ref[16 * g + 8 * h : 16 * g + 8 * h + 8, :] * picks[g] for g in range(16)]
+        )
+        turns = [pltpu.roll(total, shift, 1) for shift in (32, 64, 96)]
+        out.append((total + turns[0]) + (turns[1] + turns[2]))
+    return out
 
 
 def kernel(
@@ -224,7 +246,8 @@
         ).astype(bf16)
         return carry
 
-    lax.fori_loop(0, 8, pack, 0)
+    for b in range(8):
+        pack(b, 0)
 
     coef = jnp.broadcast_to(coef_ref[...], (8, coef_ref.shape[1])).astype(bf16)
     for c in range(chunks):
@@ -303,13 +326,20 @@
         sel = onehot(iota((128, 1024), 0) + 128 * h == slot_line)
         padded[128 * h : 128 * h + 128, :] = dot(sel, rows_src[...]).astype(bf16)
 
-    low = iota((32, 128), 1) < 64
-    for h in range(4):
-        pair = padded[128 * h : 128 * h + 128, :]
-        prod = dot_nt(pair, pair)
-        turned = pltpu.roll(prod, 64, 1)
-        gram[pl.ds(2 * h, 32, stride=8), :] = jnp.where(low, prod[0:32], turned[32:64])
-        gram[pl.ds(2 * h + 1, 32, stride=8), :] = jnp.where(low, turned[64:96], prod[96:128])
+    quarter = iota((16, 128), 1) >> 5
+    for m in range(8):
+        first = 64 * (m % 2)
+        if first == 0:
+            pair = padded[64 * m : 64 * m + 128, :]
+            prod = dot_nt(pair, pair)
+        for h in range(2):
+            piece = None
+            for r in range(4):
+                shift = (32 * r - first - 32 * h) % 128
+                lines = prod[first + 16 * r : first + 16 * r + 16]
+                lines = pltpu.roll(lines, shift, 1) if shift else lines
+                piece = lines if piece is None else jnp.where(quarter == r, lines, piece)
+            gram[pl.ds(8 * h + m, 16, stride=16), :] = piece
 
     marks = jnp.concatenate(
         [jnp.where(mine, line(label_in).astype(f32), 0.0), jnp.where(mine, 1.0, 0.0)], axis=0
@@ -328,25 +358,39 @@
     offset = fold3(dot_nt(stack3(jnp.where(mine, score_line, 0.0)), bhot[...]))
 
     lane = iota((8, 128), 1)
-    low = lane < 64
+
+    def halves(x):
+        return [take(x, (lane & 31) + 32 * h) for h in range(2)]
+
+    def joined(v):
+        return jnp.where((lane >> 5) & 1 == 0, v[0], v[1])
+
+    offset, live, label, start = halves(offset), halves(live), halves(label), halves(start)
 
     def newton(step, carry):
-        u, _ = carry
-        prob = jax.nn.sigmoid(offset + u)
-        slope = live * (prob - label)
-        root = jnp.sqrt(live * prob * (1.0 - prob))
-        rhs = root * (gram_times(gram, slope) + u)
+        u = carry[0:2]
+        prob = [jax.nn.sigmoid(offset[h] + u[h]) for h in range(2)]
+        slope = [live[h] * (prob[h] - label[h]) for h in range(2)]
+        root = [jnp.sqrt(live[h] * prob[h] * (1.0 - prob[h])) for h in range(2)]
+        pull = gram_times(gram, slope)
         rows = []
-        for p in range(32):
-            scaled = gram[8 * p : 8 * p + 8, :] * root * take(root, jnp.where(low, p, p + 32))
-            diagonal = (lane == p) | (lane == p + 96)
-            rows.append(scaled + jnp.where(diagonal, 1.0, 0.0))
-        beta = root * solve(rows, rhs) - slope
-        return gram_times(gram, beta), beta
-
-    value, beta = lax.fori_loop(0, NEWTON, newton, (start, jnp.zeros((8, 128), f32)))
-
-    back = fold3(dot(stack3(jnp.where(low, value, 0.0)), bhot[...]))
+        for g in range(16):
+            across = by_rows(root, g)
+            pair = []
+            for h in range(2):
+                scaled = gram[16 * g + 8 * h : 16 * g + 8 * h + 8, :] * root[h] * across
+                diagonal = 16 * (lane >> 5) + g == 32 * h + (lane & 31)
+                pair.append(scaled + jnp.where(diagonal, 1.0, 0.0))
+            rows.append(pair)
+        solved = solve(rows, [root[h] * (pull[h] + u[h]) for h in range(2)])
+        beta = [root[h] * solved[h] - slope[h] for h in range(2)]
+        return tuple(gram_times(gram, beta)) + tuple(beta)
+
+    zero = jnp.zeros((8, 128), f32)
+    final = lax.fori_loop(0, NEWTON, newton, tuple(start) + (zero, zero))
+    value, beta = joined(final[0:2]), joined(final[2:4])
+
+    back = fold3(dot(stack3(jnp.where(lane < 64, value, 0.0)), bhot[...]))
     back = jnp.sum(jnp.where(mine, back, 0.0), axis=0, keepdims=True)
     for a in range(8):
         bk[a] = back[:, 128 * a : 128 * a + 128]

time: 38.3 us -> 38.7 us (1.010)
  Pallas kernels: 37.5 us -> 37.9 us
where the time goes in v4:
time: 38.7 us; the launch traced here: 38.5 us
  Pallas kernels  37.9 us (98%)
  between operations  0.64 us (2%)
    pallas_call x1, Pallas kernels, per_device(): pl.pallas_call(kernel, name='glmix', out_shape=pltpu.VMEM((16, 256), f32)...  37.3 us

profile of v4, /device:TPU:1, one launch (start us, length us, event | category | flops | bytes accessed | tf_op | source)
XLA Modules:
  0.0 38.5 jit_solution(3416485103723965207)
XLA Ops:
  0.6 37.3 %glmix.1.merged_ref = f32[16,256]{1,0:T(8,128)S(1)} custom-call(f32[1,512]{1,0:T(1,128)} %bitcast.8, f32[32,128]{1,0:T(8,128)} %bitcast.6, s32[32,128]{1,0:T(8,128)} %bitcast.7, bf16[256,256]{1,0:T(8,128)(2,1)} %mfeat_hbm.1, f32[8,256]{1,0:T(8,128)} %mcoef_hbm.1, s32[1,256]{1,0:T(1,128)} %bitcast.9, bf16[4096,512]{1,0:T(8,128)(2,1)} %feat_ref.1), custom_call_target="tpu_custom_call" | custom-call | tf_op jit(solution)/shard_map/glmix/pallas_call | solution.py:460
  37.9 0.6 %split.1 = (f32[1,512]{1,0:T(1,128)}, f32[8,256]{1,0:T(8,128)}, f32[1,256]{1,0:T(1,128)}) custom-call(f32[16,256]{1,0:T(8,128)S(1)} %glmix.1.merged_ref), custom_call_target="tpu_custom_call" | custom-call | tf_op jit(solution)/shard_map/split/pallas_call | solution.py:507

commit v5 on v4

--- a/solution.py
+++ b/solution.py
@@ -7,7 +7,7 @@
 from jax.experimental.pallas import tpu as pltpu
 from jax.sharding import PartitionSpec as P
 
-SPLIT = 104
+SPLIT = 84
 LOGICAL = pl.DeviceIdType.LOGICAL
 BLK = 64
 NEWTON = 3

time: 38.7 us -> 36.4 us (0.941)
  Pallas kernels: 37.9 us -> 35.7 us
    pallas_call x1, Pallas kernels: 37.3 us -> 35.1 us  [per_device(): pl.pallas_call(kernel, name='glmix', out_shape=pltpu.VMEM((16, 256), f32)...]
where the time goes in v5:
time: 36.4 us; the launch traced here: 36.3 us
  Pallas kernels  35.7 us (98%)
  between operations  0.64 us (2%)
    pallas_call x1, Pallas kernels, per_device(): pl.pallas_call(kernel, name='glmix', out_shape=pltpu.VMEM((16, 256), f32)...  35.1 us

profile of v5, /device:TPU:1, one launch (start us, length us, event | category | flops | bytes accessed | tf_op | source)
XLA Modules:
  0.0 36.3 jit_solution(15380098831285467874)
XLA Ops:
  0.6 35.1 %glmix.1.merged_ref = f32[16,256]{1,0:T(8,128)S(1)} custom-call(f32[1,512]{1,0:T(1,128)} %bitcast.8, f32[32,128]{1,0:T(8,128)} %bitcast.6, s32[32,128]{1,0:T(8,128)} %bitcast.7, bf16[256,256]{1,0:T(8,128)(2,1)} %mfeat_hbm.1, f32[8,256]{1,0:T(8,128)} %mcoef_hbm.1, s32[1,256]{1,0:T(1,128)} %bitcast.9, bf16[4096,512]{1,0:T(8,128)(2,1)} %feat_ref.1), custom_call_target="tpu_custom_call" | custom-call | tf_op jit(solution)/shard_map/glmix/pallas_call | solution.py:460
  35.7 0.6 %split.1 = (f32[1,512]{1,0:T(1,128)}, f32[8,256]{1,0:T(8,128)}, f32[1,256]{1,0:T(1,128)}) custom-call(f32[16,256]{1,0:T(8,128)S(1)} %glmix.1.merged_ref), custom_call_target="tpu_custom_call" | custom-call | tf_op jit(solution)/shard_map/split/pallas_call | solution.py:507

commit v6 on v5

--- a/solution.py
+++ b/solution.py
@@ -83,34 +83,22 @@
             own = [jnp.where(inside, 0.0, x) for x in own]
             own[v // 32] = jnp.where(side == v % 32, 1.0, own[v // 32])
             t.append(own)
-        invs, factor = {}, {}
-        for k in range(0, n, 2):
-            a, b, c = block[k, k], block[k, k + 1], block[k + 1, k + 1]
-            scale = 1.0 / (a * c - b * b)
-            invs[k] = (c * scale, b * scale, a * scale)
-            for i in range(k + 2, n):
-                factor[i, k] = (c * block[k, i] - b * block[k + 1, i]) * scale
-                factor[i, k + 1] = (a * block[k + 1, i] - b * block[k, i]) * scale
-            for i in range(k + 2, n):
+        inv, factor = [], {}
+        for k in range(n):
+            inv.append(1.0 / block[k, k])
+            for i in range(k + 1, n):
+                factor[i, k] = block[k, i] * inv[k]
+            for i in range(k + 1, n):
                 for j in range(i, n):
-                    block[i, j] = block[i, j] - (
-                        factor[i, k] * block[k, j] + factor[i, k + 1] * block[k + 1, j]
-                    )
+                    block[i, j] = block[i, j] - factor[i, k] * block[k, j]
                 for h in range(2):
-                    t[i][h] = t[i][h] - (
-                        factor[i, k] * t[k][h] + factor[i, k + 1] * t[k + 1][h]
-                    )
-        for k in range(0, n, 2):
-            a, b, c = invs[k]
-            for h in range(2):
-                t[k][h], t[k + 1][h] = (
-                    a * t[k][h] - b * t[k + 1][h],
-                    c * t[k + 1][h] - b * t[k][h],
-                )
-        for k in range(n - 2, 0, -2):
+                    t[i][h] = t[i][h] - factor[i, k] * t[k][h]
+        for i in range(n):
+            t[i] = [x * inv[i] for x in t[i]]
+        for k in range(n - 1, 0, -1):
             for i in range(k):
                 for h in range(2):
-                    t[i][h] = t[i][h] - (factor[k, i] * t[k][h] + factor[k + 1, i] * t[k + 1][h])
+                    t[i][h] = t[i][h] - factor[k, i] * t[k][h]
         step = [tree_sum([ys[i] * t[i][h] for i in range(n)]) for h in range(2)]
         s = [s[h] + jnp.where(done, step[h], 0.0) for h in range(2)]
         y = [y[h] - jnp.where(done, 0.0, step[h]) for h in range(2)]
@@ -120,8 +108,10 @@
             ]
             for at_, g in enumerate(part):
                 for h in range(2):
-                    change = tree_sum([picks[i][at_] * t[i][h] for i in range(n)])
-                    rows[g][h] = jnp.where(inside, 0.0, rows[g][h]) - change
+                    kept = jnp.where(inside, 0.0, rows[g][h])
+                    for i in range(n):
+                        kept = kept - picks[i][at_] * t[i][h]
+                    rows[g][h] = kept
     return s
 
 
@@ -269,6 +259,10 @@
     rin[me] = msg[me]
 
     arrived(rs.at[pl.ds(0, n_feat - 1)], 0)
+    for a, b in all_far[SPLIT:105]:
+        t = dps[a] * n_feat + feats[b]
+        send(msg.at[t], rin.at[me], 1, t).start()
+
     score = rs[0]
     for f in range(1, n_feat):
         score = score + rs[f]
@@ -286,7 +280,7 @@
         t = dps[a] * n_feat + feats[b]
         send(sc.at[t], scr.at[me], 2, t).start()
 
-    for a, b in all_far[SPLIT:]:
+    for a, b in all_far[105:]:
         t = dps[a] * n_feat + feats[b]
         send(msg.at[t], rin.at[me], 1, t).start()
 
@@ -438,8 +432,7 @@
     arrived(ret.at[pl.ds(0, n_dev - 1)], 5)
     lane_half = onehot(iota((128, 256), 0) == lane_of[...])
     came = ret[...].reshape(n_dev, 128)
-    got = [dot(t, lane_half) for t in split3(came)]
-    got = (got[0] + got[1]) + got[2]
+    got = dot(jnp.concatenate(split3(came), axis=1), jnp.concatenate([lane_half] * 3, axis=0))
     mine_back = jnp.sum(jnp.where(iota((n_dev, 256), 0) == slot_ref[...] >> 9, got, 0.0), axis=0)
     out_ref[10:11, :] = own[...] + mine_back[None, :]
     sent(ret.at[pl.ds(0, n_dev - 1)], 5)

time: 36.4 us -> 36 us (0.989)
  Pallas kernels: 35.7 us -> 35.3 us
    pallas_call x1, Pallas kernels: 35.1 us -> 34.7 us  [per_device(): pl.pallas_call(kernel, name='glmix', out_shape=pltpu.VMEM((16, 256), f32)...]
where the time goes in v6:
time: 36 us; the launch traced here: 35.9 us
  Pallas kernels  35.3 us (98%)
  between operations  0.64 us (2%)
    pallas_call x1, Pallas kernels, per_device(): pl.pallas_call(kernel, name='glmix', out_shape=pltpu.VMEM((16, 256), f32)...  34.7 us

profile of v6, /device:TPU:1, one launch (start us, length us, event | category | flops | bytes accessed | tf_op | source)
XLA Modules:
  0.0 35.9 jit_solution(18035294133439500019)
XLA Ops:
  0.6 34.7 %glmix.1.merged_ref = f32[16,256]{1,0:T(8,128)S(1)} custom-call(f32[1,512]{1,0:T(1,128)} %bitcast.8, f32[32,128]{1,0:T(8,128)} %bitcast.6, s32[32,128]{1,0:T(8,128)} %bitcast.7, bf16[256,256]{1,0:T(8,128)(2,1)} %mfeat_hbm.1, f32[8,256]{1,0:T(8,128)} %mcoef_hbm.1, s32[1,256]{1,0:T(1,128)} %bitcast.9, bf16[4096,512]{1,0:T(8,128)(2,1)} %feat_ref.1), custom_call_target="tpu_custom_call" | custom-call | tf_op jit(solution)/shard_map/glmix/pallas_call | solution.py:453
  35.3 0.6 %split.1 = (f32[1,512]{1,0:T(1,128)}, f32[8,256]{1,0:T(8,128)}, f32[1,256]{1,0:T(1,128)}) custom-call(f32[16,256]{1,0:T(8,128)S(1)} %glmix.1.merged_ref), custom_call_target="tpu_custom_call" | custom-call | tf_op jit(solution)/shard_map/split/pallas_call | solution.py:500

commit v7 on v6

--- a/solution.py
+++ b/solution.py
@@ -100,6 +100,8 @@
                 for h in range(2):
                     t[i][h] = t[i][h] - factor[k, i] * t[k][h]
         step = [tree_sum([ys[i] * t[i][h] for i in range(n)]) for h in range(2)]
+        if q + GROUPS == 16:
+            return [s[h] + step[h] for h in range(2)]
         s = [s[h] + jnp.where(done, step[h], 0.0) for h in range(2)]
         y = [y[h] - jnp.where(done, 0.0, step[h]) for h in range(2)]
         for part in (range(q + GROUPS, min(q + 2 * GROUPS, 16)), range(q + 2 * GROUPS, 16)):
@@ -112,7 +114,6 @@
                     for i in range(n):
                         kept = kept - picks[i][at_] * t[i][h]
                     rows[g][h] = kept
-    return s
 
 
 def tree_sum(terms):
@@ -263,9 +264,7 @@
         t = dps[a] * n_feat + feats[b]
         send(msg.at[t], rin.at[me], 1, t).start()
 
-    score = rs[0]
-    for f in range(1, n_feat):
-        score = score + rs[f]
+    score = tree_sum([rs[f] for f in range(n_feat)])
     own[...] = score
     ag[feat] = score
     lane_hot = iota((128, 256), 0) == lane_of[...]

time: 36 us -> 36 us (level)
  no operation moved by 1% of the time
where the time goes in v7:
time: 36 us; the launch traced here: 35.9 us
  Pallas kernels  35.3 us (98%)
  between operations  0.64 us (2%)
    pallas_call x1, Pallas kernels, per_device(): pl.pallas_call(kernel, name='glmix', out_shape=pltpu.VMEM((16, 256), f32)...  34.7 us

profile of v7, /device:TPU:1, one launch (start us, length us, event | category | flops | bytes accessed | tf_op | source)
XLA Modules:
  0.0 35.9 jit_solution(2049305150439523233)
XLA Ops:
  0.6 34.7 %glmix.1.merged_ref = f32[16,256]{1,0:T(8,128)S(1)} custom-call(f32[1,512]{1,0:T(1,128)} %bitcast.8, f32[32,128]{1,0:T(8,128)} %bitcast.6, s32[32,128]{1,0:T(8,128)} %bitcast.7, bf16[256,256]{1,0:T(8,128)(2,1)} %mfeat_hbm.1, f32[8,256]{1,0:T(8,128)} %mcoef_hbm.1, s32[1,256]{1,0:T(1,128)} %bitcast.9, bf16[4096,512]{1,0:T(8,128)(2,1)} %feat_ref.1), custom_call_target="tpu_custom_call" | custom-call | tf_op jit(solution)/shard_map/glmix/pallas_call | solution.py:452
  35.3 0.6 %split.1 = (f32[1,512]{1,0:T(1,128)}, f32[8,256]{1,0:T(8,128)}, f32[1,256]{1,0:T(1,128)}) custom-call(f32[16,256]{1,0:T(8,128)S(1)} %glmix.1.merged_ref), custom_call_target="tpu_custom_call" | custom-call | tf_op jit(solution)/shard_map/split/pallas_call | solution.py:499
